TPU v7x, 32 devices: a whole 2x2x4 slice. The times are simulated.
32 devices in a mesh: dp: 8 (over y, x, core), tensor: 4 (over z).
Axes of the slice: x: 2, y: 2, z: 4, core: 2. Of those that a mesh axis runs over, the one named last changes fastest.
Arguments:
- wq_flat: bfloat16 [8192, 4096], P(('dp', 'tensor')), may hold values from -0.125 to 0.125
- hidden: bfloat16 [4, 16, 8192], P(None, 'dp'), may hold values from -6 to 6
- cache: bfloat16 [16, 4, 8192, 256], P('dp', None, 'tensor'), may hold values from -300 to 300
- new_kv: bfloat16 [4, 16, 4, 256], P(None, 'dp'), may hold values from -6 to 6
- lengths: int32 [16], P('dp'), may hold values from 1 to 8192, as said below
Outputs:
- attended: bfloat16 [4, 16, 4096], P(None, 'dp', 'tensor')
Inputs may be any that keep to these rules, and one draw needn't show every extreme that they name: `lengths`: every sequence has at least one cached position; in every draw some sequence has exactly 8192.
All inputs are finite; a program needn't handle non-finite values.
Results may differ from a plain program's by a relative error of at most 0.03.
Values may be sent and summed in bfloat16 or wider, within the bound.
A program may use at most 64 MiB of HBM per device.

v0:
```python
import jax
import jax.numpy as jnp
from jax import lax
from jax.sharding import PartitionSpec as P

QH = 32
HD = 128


def merged(shard, axis, combine):
    everything = jax.tree.map(lambda part: lax.all_gather(part, axis), shard)
    initial = jax.tree.map(lambda part: part[0], everything)

    def step(k, so_far):
        return combine(so_far, jax.tree.map(lambda part: part[k], everything))

    return lax.fori_loop(1, lax.axis_size(axis), step, initial)


def combine_parts(first, second):
    best = jnp.maximum(first[0], second[0])
    scale_one = jnp.exp(first[0] - best)
    scale_two = jnp.exp(second[0] - best)
    total = first[1] * scale_one + second[1] * scale_two
    accum = first[2] * scale_one[..., None] + second[2] * scale_two[..., None]
    return (best, total, accum)


def body(wq_flat, hidden, cache, new_kv, lengths):
    n_tensor = lax.axis_size("tensor")
    n_replica = lax.axis_size("dp")
    rank = lax.axis_index("tensor")
    steps, seq_dev, width = hidden.shape
    kv_heads = cache.shape[1]
    ctx_dev = cache.shape[2]
    group = QH // kv_heads
    heads_dev = QH // n_tensor
    scale = 1.0 / HD**0.5
    rows = steps * seq_dev
    flat_rows = hidden.reshape(rows, width)
    shard_rows = wq_flat.shape[0]
    blocks = flat_rows.reshape(rows, n_replica, n_tensor, shard_rows)
    picked = lax.dynamic_index_in_dim(blocks, rank, 2, keepdims=False).reshape(
        rows, n_replica * shard_rows
    )
    partial_value = jnp.dot(
        picked,
        lax.all_gather(wq_flat, "dp", axis=0, tiled=True),
        preferred_element_type=jnp.float32,
    )
    query_all = lax.psum(partial_value, "tensor").astype(jnp.bfloat16)
    query_own = lax.dynamic_slice_in_dim(query_all, rank * heads_dev * HD, heads_dev * HD, 1)
    queries = query_all.reshape(steps, seq_dev, kv_heads, group, HD)
    keys = cache[..., :HD]
    values = cache[..., HD:]
    scores = (
        jnp.einsum("tsgjd,sgcd->gjtsc", queries, keys, preferred_element_type=jnp.float32) * scale
    )
    positions = rank * ctx_dev + jnp.arange(ctx_dev)
    valid = (positions[None, :] < lengths[:, None])[None, None, None, :, :]
    masked = jnp.where(valid, scores, -1e30)
    local_max = jnp.max(masked, axis=-1)
    weights = jnp.where(valid, jnp.exp(masked - local_max[..., None]), 0.0)
    local_total = jnp.sum(weights, axis=-1)
    local_acc = jnp.einsum(
        "gjtsc,sgcd->gjtsd",
        weights.astype(jnp.bfloat16),
        values,
        preferred_element_type=jnp.float32,
    )
    local_max = local_max.reshape(QH, steps, seq_dev)
    local_total = local_total.reshape(QH, steps, seq_dev)
    local_acc = local_acc.reshape(QH, steps, seq_dev, HD)
    best, denom, accum = merged((local_max, local_total, local_acc), "tensor", combine_parts)
    best = lax.dynamic_slice_in_dim(best, rank * heads_dev, heads_dev, 0)
    denom = lax.dynamic_slice_in_dim(denom, rank * heads_dev, heads_dev, 0)
    accum = lax.dynamic_slice_in_dim(accum, rank * heads_dev, heads_dev, 0)
    kv_index = rank * heads_dev // group
    fresh = lax.dynamic_slice_in_dim(new_kv, kv_index, 1, 2)[:, :, 0, :]
    own_q = query_own.reshape(steps, seq_dev, heads_dev, HD)
    new_scores = (
        jnp.einsum("tsjd,usd->jtsu", own_q, fresh[..., :HD], preferred_element_type=jnp.float32)
        * scale
    )
    causal = (jnp.arange(steps)[:, None] >= jnp.arange(steps)[None, :])[None, :, None, :]
    new_masked = jnp.where(causal, new_scores, -1e30)
    top = jnp.maximum(best, jnp.max(new_masked, axis=-1))
    old_scale = jnp.exp(best - top)
    new_weights = jnp.where(causal, jnp.exp(new_masked - top[..., None]), 0.0)
    denom = denom * old_scale + jnp.sum(new_weights, axis=-1)
    accum = accum * old_scale[..., None] + jnp.einsum(
        "jtsu,usd->jtsd",
        new_weights.astype(jnp.bfloat16),
        fresh[..., HD:],
        preferred_element_type=jnp.float32,
    )
    result = accum / denom[..., None]
    return result.transpose(1, 2, 0, 3).reshape(steps, seq_dev, heads_dev * HD).astype(jnp.bfloat16)


def solution(mesh):
    placed = (
        P(("dp", "tensor"), None),
        P(None, "dp", None),
        P("dp", None, "tensor", None),
        P(None, "dp", None, None),
        P("dp"),
    )
    return jax.shard_map(
        body, mesh=mesh, in_specs=placed, out_specs=P(None, "dp", "tensor"), check_vma=False
    )
```

profile of v0, /device:TPU:0, one launch (start us, length us, event | category | flops | bytes accessed | tf_op | source)
XLA Modules:
  0.0 189.2 jit_solution(12184188657150206391)
XLA Ops:
  6.5 0.7 all-gather.2.cloned.1.call-update
  7.3 0.2 copy-done.2
  7.5 0.1 reshape_reshape.3
  7.6 0.2 dynamic-slice_reduce_fusion
  8.0 5.8 %fusion.34 = (bf16[2,4,2048,128]{3,2,1,0:T(8,128)(2,1)}, bf16[2,4,2048,128]{3,2,1,0:T(8,128)(2,1)}) fusion(bf16[2,4,2048,256]{3,2,1,0:T(8,128)(2,1)} %param.9), kind=kLoop, calls=%fused_computation.61 | loop fusion | bytes 16777216 | tf_op jit(solution)/shard_map/slice | solution.py:55
  13.7 88.0 %all-gather.2.cloned.1.call-done = bf16[2048,4096]{1,0:T(8,128)(2,1)} async-done(((bf16[256,4096]{1,0:T(8,128)(2,1)}), bf16[2048,4096]{1,0:T(8,128)(2,1)}) %all-gather.2.cloned.1.call-update) | async-done | bytes 16777232 | tf_op jit(solution)/shard_map/all_gather | solution.py:48
  101.7 8.0 %fusion.37 = f32[8,4096]{1,0:T(8,128)S(1)} fusion(bf16[8,2048]{1,0:T(8,128)(2,1)S(1)} %bitcast.110, bf16[2048,4096]{1,0:T(8,128)(2,1)} %all-gather.2.cloned.1.call-done), kind=kOutput, calls=%fused_computation.64 | convolution fusion | flops 134217728 | bytes 16941056 | tf_op jit(solution)/shard_map/dot_general | solution.py:46
  109.7 21.2 %all-reduce.1 = bf16[8,4096]{1,0:T(8,128)(2,1)S(1)} all-reduce(f32[8,4096]{1,0:T(8,128)S(1)} %fusion.37), channel_id=1, replica_groups=mesh['dp'=8,'tensor'=4] {'tensor'}, use_global_device_ids=true, to_apply=%region_0.1 | all-reduce | flops 32768 | bytes 196608 | tf_op jit(solution)/shard_map/psum | solution.py:51
  130.9 3.9 %fusion.35 = (f32[4,8,4,2]{1,2,3,0:T(4,128)S(1)}, f32[4,8,4,2,2048]{4,1,2,3,0:T(8,128)S(1)}) fusion(bf16[2,4,2048,128]{3,2,1,0:T(8,128)(2,1)} %get-tuple-element.230, bf16[4,2,4,8,128]{4,3,2,1,0:T(8,128)(2,1)S(1)} %bitcast.109, pred[2,2048]{1,0:T(4,128)(4,1)S(1)} %broadcast_compare_fusion), kind=kOutput, calls=%fused_computation.62 | convolution fusion | flops 135790336 | bytes 6362112 | tf_op jit(solution)/shard_map/tsgjd,sgcd->gjtsc/dot_general | solution.py:57
  134.9 0.5 fusion.11
  135.4 0.8 fusion.12
  136.2 14.7 %all_gather.15 = f32[4,32,4,2,128]{4,1,3,2,0:T(8,128)S(1)} all-gather(f32[1,32,4,2,128]{4,1,3,2,0:T(8,128)S(1)} %bitcast.107), channel_id=1, replica_groups=mesh['dp'=8,'tensor'=4] {'tensor'}, dimensions={0}, use_global_device_ids=true | all-gather | bytes 655360 | tf_op jit(solution)/shard_map/all_gather | solution.py:11
  150.9 0.1 copy.67
  151.0 0.1 reshape.67
  151.1 13.2 %all_gather.14 = f32[4,32,4,2]{1,2,3,0:T(4,128)S(1)} all-gather(f32[1,32,4,2]{1,2,3,0:T(4,128)S(1)} %reshape.67), channel_id=1, replica_groups=mesh['dp'=8,'tensor'=4] {'tensor'}, dimensions={0}, use_global_device_ids=true | all-gather | bytes 5120 | tf_op jit(solution)/shard_map/all_gather | solution.py:11
  164.3 0.1 all_gather_reshape.9
  164.4 13.2 %all_gather.13 = f32[4,32,4,2]{1,2,3,0:T(4,128)S(1)} all-gather(f32[1,32,4,2]{1,2,3,0:T(4,128)S(1)} %all_gather_reshape.9), channel_id=1, replica_groups=mesh['dp'=8,'tensor'=4] {'tensor'}, dimensions={0}, use_global_device_ids=true | all-gather | bytes 5120 | tf_op jit(solution)/shard_map/all_gather | solution.py:11
  177.6 3.3 %while.19 = (s32[]{:T(128)}, f32[32,4,2]{0,2,1:T(2,128)S(1)}, f32[32,4,2]{0,2,1:T(2,128)S(1)}, f32[32,4,2,128]{3,2,1,0:T(2,128)S(1)}, f32[4,32,4,2]{1,2,3,0:T(4,...) while((s32[]{:T(128)}, f32[32,4,2]{0,2,1:T(2,128)S(1)}, ...), condition=%wide.region_4.5_spmd, body=%wide.region_3.4_spmd.sunk | while | flops 99845 | bytes 673943 | solution.py:17
  177.7 0.1 copy.141
  177.8 0.1 copy.142
  177.9 0.8 fusion.43
  178.8 0.1 copy.141
  178.9 0.1 copy.142
  179.0 0.8 fusion.43
  179.9 0.1 copy.141
  180.0 0.1 copy.142
  180.1 0.8 fusion.43
  181.0 0.2 fusion.36
  181.3 0.1 fusion.25
  181.4 0.1 multiply_add_fusion
  181.5 0.3 fusion.16
  181.8 0.6 copy.76
  (39 shorter events, 0.5 us)
Async XLA Ops:
  6.5 1.3 copy-start
  6.5 0.9 copy-start.2
  6.5 1.3 copy-start.3
  6.5 95.2 %all-gather.2.cloned.1.call-start = ((), (), s32[]{:S(2)}) async-start(), calls=%async_computation | async-start | bytes 18874368 | tf_op jit(solution)/shard_map/all_gather | solution.py:48
  130.9 4.4 %copy-start.1 = (bf16[2,4,2048,128]{3,2,1,0:T(8,128)(2,1)S(1)}, bf16[2,4,2048,128]{3,2,1,0:T(8,128)(2,1)}, u32[]{:S(2)}) copy-start(bf16[2,4,2048,128]{3,2,1,0:T(8,128)(2,1)} %get-tuple-element.229) | copy-start | bytes 12582916
Sparse Core Ops, SparseCore 0:
  9.2 92.4 all-gather.1
where the time goes:
time: 189 us
  waiting for transfers between devices  88.7 us (47%)
  blocking collectives  62.2 us (33%)
  between operations  13.6 us (7%)
  matrix products  13.2 us (7%)
  local copies, waits for them, and re-layouts  8.06 us (4%)
  other arithmetic  3.33 us (2%)
    all_gather x1, waiting for transfers between devices, body(): lax.all_gather(wq_flat, 'dp', axis=0, tiled=True)  88 us
    all_gather x3, blocking collectives, merged(): everything = jax.tree.map(lambda part: lax.all_gather(part, axis), shard)  41.1 us
    psum x1, blocking collectives, body(): query_all = lax.psum(partial_value, 'tensor').astype(jnp.bfloat16)  21.2 us
    dot_general x1, matrix products, body(): jnp.dot(picked, lax.all_gather(wq_flat, 'dp', axis=0, tiled=True), prefer...  8.04 us
    slice x1, local copies, waits for them, and re-layouts, body(): values = cache[..., HD:]  5.76 us
    dot_general x1, matrix products, body(): jnp.einsum('tsgjd,sgcd->gjtsc', queries, keys, preferred_element_type=jnp...  3.89 us
  transfers between devices with their start and end apart: 1, of which 1 were waited for; matrix products, arithmetic and copies ran while one was open for 3% of the time, Pallas kernels for 0%

commit v1 on v0

--- a/solution.py
+++ b/solution.py
@@ -48,7 +48,7 @@
         lax.all_gather(wq_flat, "dp", axis=0, tiled=True),
         preferred_element_type=jnp.float32,
     )
-    query_all = lax.psum(partial_value, "tensor").astype(jnp.bfloat16)
+    query_all = jnp.sum(lax.all_gather(partial_value, "tensor"), axis=0).astype(jnp.bfloat16)
     query_own = lax.dynamic_slice_in_dim(query_all, rank * heads_dev * HD, heads_dev * HD, 1)
     queries = query_all.reshape(steps, seq_dev, kv_heads, group, HD)
     keys = cache[..., :HD]

time: 189 us -> 184 us (0.974)
  blocking collectives: 62.2 us -> 58.5 us
  matrix products: 13.2 us -> 11 us
    psum x1 -> x0, blocking collectives: 21.2 us -> none  [body(): query_all = lax.psum(partial_value, 'tensor').astype(jnp.bfloat16)]
    all_gather x0 -> x1, blocking collectives: none -> 16 us  [body(): lax.all_gather(partial_value, 'tensor')]
    dot_general x1, matrix products: 3.89 us -> 1.55 us  [body(): jnp.einsum('tsgjd,sgcd->gjtsc', queries, keys, preferred_element_type=jnp...]
where the time goes in v1:
time: 184 us; the launch traced here: 183 us
  waiting for transfers between devices  88.7 us (48%)
  blocking collectives  58.5 us (32%)
  between operations  13.6 us (7%)
  matrix products  11 us (6%)
  local copies, waits for them, and re-layouts  8.15 us (4%)
  other arithmetic  3.36 us (2%)
    all_gather x1, waiting for transfers between devices, body(): lax.all_gather(wq_flat, 'dp', axis=0, tiled=True)  88 us
    all_gather x3, blocking collectives, merged(): everything = jax.tree.map(lambda part: lax.all_gather(part, axis), shard)  42.5 us
    all_gather x1, blocking collectives, body(): lax.all_gather(partial_value, 'tensor')  16 us
    dot_general x1, matrix products, body(): jnp.dot(picked, lax.all_gather(wq_flat, 'dp', axis=0, tiled=True), prefer...  8.19 us
    slice x1, local copies, waits for them, and re-layouts, body(): values = cache[..., HD:]  5.76 us
  transfers between devices with their start and end apart: 1, of which 1 were waited for; matrix products, arithmetic and copies ran while one was open for 3% of the time, Pallas kernels for 0%

profile of v1, /device:TPU:0, one launch (start us, length us, event | category | flops | bytes accessed | tf_op | source)
XLA Modules:
  0.0 183.4 jit_solution(15900646164038380893)
XLA Ops:
  6.5 0.7 all-gather.3.cloned.1.call-update
  7.3 0.2 copy-done.3
  7.5 0.1 reshape_reshape.3
  7.6 0.2 dynamic-slice_reduce_fusion
  8.0 5.8 %fusion.34 = (bf16[2,4,2048,128]{3,2,1,0:T(8,128)(2,1)}, bf16[2,4,2048,128]{3,2,1,0:T(8,128)(2,1)}) fusion(bf16[2,4,2048,256]{3,2,1,0:T(8,128)(2,1)} %param.9), kind=kLoop, calls=%fused_computation.62 | loop fusion | bytes 16777216 | tf_op jit(solution)/shard_map/slice | solution.py:55
  13.7 88.0 %all-gather.3.cloned.1.call-done = bf16[2048,4096]{1,0:T(8,128)(2,1)} async-done(((bf16[256,4096]{1,0:T(8,128)(2,1)}), bf16[2048,4096]{1,0:T(8,128)(2,1)}) %all-gather.3.cloned.1.call-update) | async-done | bytes 16777232 | tf_op jit(solution)/shard_map/all_gather | solution.py:48
  101.7 8.2 %fusion.37 = f32[8,4096]{1,0:T(8,128)S(1)} fusion(bf16[8,2048]{1,0:T(8,128)(2,1)S(1)} %bitcast.112, bf16[2048,4096]{1,0:T(8,128)(2,1)} %all-gather.3.cloned.1.call-done), kind=kOutput, calls=%fused_computation.65 | convolution fusion | flops 134217728 | bytes 16941056 | tf_op jit(solution)/shard_map/dot_general | solution.py:46
  109.9 16.0 %all-gather = f32[32,4096]{1,0:T(8,128)S(1)} all-gather(f32[8,4096]{1,0:T(8,128)S(1)} %fusion.37), channel_id=2, replica_groups=mesh['dp'=8,'tensor'=4] {'tensor'}, dimensions={0}, use_global_device_ids=true | all-gather | bytes 655360 | tf_op jit(solution)/shard_map/all_gather | solution.py:51
  126.0 1.6 fusion.35
  127.6 0.5 fusion.11
  128.1 0.1 copy-done.2
  128.2 0.8 fusion.12
  129.0 16.1 %all_gather.23 = f32[4,32,4,2,128]{4,1,3,2,0:T(8,128)S(1)} all-gather(f32[1,32,4,2,128]{4,1,3,2,0:T(8,128)S(1)} %bitcast.109), channel_id=1, replica_groups=mesh['dp'=8,'tensor'=4] {'tensor'}, dimensions={0}, use_global_device_ids=true | all-gather | bytes 655360 | tf_op jit(solution)/shard_map/all_gather | solution.py:11
  145.1 0.1 copy.66
  145.2 0.1 reshape.67
  145.3 13.2 %all_gather.22 = f32[4,32,4,2]{1,2,3,0:T(4,128)S(1)} all-gather(f32[1,32,4,2]{1,2,3,0:T(4,128)S(1)} %reshape.67), channel_id=1, replica_groups=mesh['dp'=8,'tensor'=4] {'tensor'}, dimensions={0}, use_global_device_ids=true | all-gather | bytes 5120 | tf_op jit(solution)/shard_map/all_gather | solution.py:11
  158.5 0.1 all_gather_reshape.9
  158.6 13.2 %all_gather.21 = f32[4,32,4,2]{1,2,3,0:T(4,128)S(1)} all-gather(f32[1,32,4,2]{1,2,3,0:T(4,128)S(1)} %all_gather_reshape.9), channel_id=1, replica_groups=mesh['dp'=8,'tensor'=4] {'tensor'}, dimensions={0}, use_global_device_ids=true | all-gather | bytes 5120 | tf_op jit(solution)/shard_map/all_gather | solution.py:11
  171.8 3.3 %while.19 = (s32[]{:T(128)}, f32[32,4,2]{0,2,1:T(2,128)S(1)}, f32[32,4,2]{0,2,1:T(2,128)S(1)}, f32[32,4,2,128]{3,2,1,0:T(2,128)S(1)}, f32[4,32,4,2]{1,2,3,0:T(4,...) while((s32[]{:T(128)}, f32[32,4,2]{0,2,1:T(2,128)S(1)}, ...), condition=%wide.region_4.5_spmd, body=%wide.region_3.4_spmd.sunk | while | flops 99845 | bytes 673943 | solution.py:17
  171.9 0.1 copy.140
  172.0 0.1 copy.141
  172.1 0.8 fusion.43
  173.0 0.1 copy.140
  173.1 0.1 copy.141
  173.2 0.8 fusion.43
  174.1 0.1 copy.140
  174.2 0.1 copy.141
  174.3 0.8 fusion.43
  175.2 0.2 fusion.36
  175.5 0.1 fusion.25
  175.7 0.3 fusion.16
  176.0 0.6 copy.75
  (42 shorter events, 0.6 us)
Async XLA Ops:
  6.5 1.3 copy-start
  6.5 0.9 copy-start.3
  6.5 1.3 copy-start.4
  6.5 95.2 %all-gather.3.cloned.1.call-start = ((), (), s32[]{:S(2)}) async-start(), calls=%async_computation | async-start | bytes 18874368 | tf_op jit(solution)/shard_map/all_gather | solution.py:48
  101.7 24.3 %copy-start.1 = (bf16[2,4,2048,128]{3,2,1,0:T(8,128)(2,1)S(1)}, bf16[2,4,2048,128]{3,2,1,0:T(8,128)(2,1)}, u32[]{:S(2)}) copy-start(bf16[2,4,2048,128]{3,2,1,0:T(8,128)(2,1)} %get-tuple-element.230) | copy-start | bytes 12582916
  126.0 2.2 %copy-start.2 = (bf16[2,4,2048,128]{3,2,1,0:T(8,128)(2,1)S(1)}, bf16[2,4,2048,128]{3,2,1,0:T(8,128)(2,1)}, u32[]{:S(2)}) copy-start(bf16[2,4,2048,128]{3,2,1,0:T(8,128)(2,1)} %get-tuple-element.229) | copy-start | bytes 12582916
Sparse Core Ops, SparseCore 0:
  9.2 92.4 all-gather.2
